TPU v7x, 32 devices: a whole 2x2x4 slice. The times are simulated.
32 devices in a mesh: dp: 8 (over z, core), expert: 4 (over y, x).
Axes of the slice: x: 2, y: 2, z: 4, core: 2. Of those that a mesh axis runs over, the one named last changes fastest.
Arguments:
- embedded: bfloat16 [64, 197, 512], P(('dp', 'expert')), may hold values from -6 to 6
- cotangent: bfloat16 [64, 197, 512], P(('dp', 'expert')), may hold values from -6 to 6
- w_qkv: bfloat16 [2, 512, 1536], P(None, 'dp'), may hold values from -0.25 to 0.25
- w_proj: bfloat16 [2, 512, 512], P(None, 'dp'), may hold values from -2.5 to 2.5
- w_router: bfloat16 [2, 512, 8], P(None, 'dp'), may hold values from -0.1875 to 0.1875
- norm_gains: bfloat16 [2, 2, 512], P(None, None, 'dp'), may hold values from 0.25 to 1.75
- norm_shifts: bfloat16 [2, 2, 512], P(None, None, 'dp'), may hold values from -1 to 1
- w_first: bfloat16 [2, 8, 512, 2048], P(None, 'expert', None, 'dp'), may hold values from -0.25 to 0.25
- w_second: bfloat16 [2, 8, 2048, 512], P(None, 'expert', 'dp'), may hold values from -1 to 1
- routes: int32 [2, 64, 197, 2], P(None, ('dp', 'expert')), may hold values from 0 to 7, all different within a row; in each aligned block of 394 rows (0 to 393, 394 to 787, ..., all dimensions but the last counted through in order) at most 147 rows name the same one
Outputs:
- out_images: bfloat16 [64, 197, 512], P(('dp', 'expert'))
- grad_images: float32 [64, 197, 512], P(('dp', 'expert'))
- grad_qkv: float32 [2, 512, 1536], P(None, 'dp')
- grad_proj: float32 [2, 512, 512], P(None, 'dp')
- grad_router: float32 [2, 512, 8], P(None, 'dp')
- grad_gains: float32 [2, 2, 512], P(None, None, 'dp')
- grad_shifts: float32 [2, 2, 512], P(None, None, 'dp')
- grad_first: float32 [2, 8, 512, 2048], P(None, 'expert', None, 'dp')
- grad_second: float32 [2, 8, 2048, 512], P(None, 'expert', 'dp')
Inputs may be any that keep to these rules, and one draw needn't show every extreme that they name: `routes`: the two experts of a token differ. Among the 394 tokens of one device in one block, no expert is named by more than 147 tokens, a bound that some block reaches.
All inputs are finite; a program needn't handle non-finite values.
Results may differ from a plain program's by a relative error of at most 0.019.
Values may be sent and summed in bfloat16 or wider, within the bound.
No kernel may reach another device: no remote copies, remote signals or barrier semaphores. Data moves between devices by JAX's collectives and lax.ppermute only.
A program may use at most 192 MiB of HBM per device.

v0:
```python
import jax
import jax.numpy as jnp
from jax import lax
from jax.sharding import PartitionSpec as P

HEADS = 8
HEAD_DIM = 64
SEQ = 197
LAYERS = 2
EPSILON = 1e-06
ROOT_HALF = 0.7071067811865476
INV_ROOT_TAU = 0.3989422804014327


def layer_norm(values, scale_in, shift_in):
    center = values - jnp.mean(values, axis=-1, keepdims=True)
    variance = jnp.mean(center * center, axis=-1, keepdims=True)
    inverse = lax.rsqrt(variance + EPSILON)
    normed = center * inverse
    return (normed * scale_in + shift_in, normed, inverse)


def norm_back(grad_out, normed, inverse, scale_in):
    grad_normed = grad_out * scale_in
    first_mean = jnp.mean(grad_normed, axis=-1, keepdims=True)
    second_mean = jnp.mean(grad_normed * normed, axis=-1, keepdims=True)
    grad_in = inverse * (grad_normed - first_mean - normed * second_mean)
    return (grad_in, jnp.sum(grad_out * normed, axis=0), jnp.sum(grad_out, axis=0))


def softmax_rows(scores):
    highest = jnp.max(scores, axis=-1, keepdims=True)
    powers = jnp.exp(scores - highest)
    row_total = jnp.sum(powers, axis=-1, keepdims=True)
    return (powers / row_total, highest + jnp.log(row_total))


def gelu_value(preact):
    return 0.5 * preact * (1.0 + lax.erf(preact * ROOT_HALF))


def gelu_slope(preact):
    return (
        0.5 * (1.0 + lax.erf(preact * ROOT_HALF))
        + preact * jnp.exp(-0.5 * preact * preact) * INV_ROOT_TAU
    )


def layer_forward(
    resid, which, w_qkv, w_proj, w_router, norm_gains, norm_shifts, w_first, w_second, routes
):
    qkv_full, proj_full, router_full, gains_full, shifts_full = (
        lax.all_gather(w_qkv[which], "dp", axis=0, tiled=True),
        lax.all_gather(w_proj[which], "dp", axis=0, tiled=True),
        lax.all_gather(w_router[which], "dp", axis=0, tiled=True),
        lax.all_gather(norm_gains[which], "dp", axis=1, tiled=True),
        lax.all_gather(norm_shifts[which], "dp", axis=1, tiled=True),
    )
    first_full, second_full = (
        lax.all_gather(w_first[which], "dp", axis=2, tiled=True),
        lax.all_gather(w_second[which], "dp", axis=1, tiled=True),
    )
    tok_count, width = resid.shape
    images = tok_count // SEQ
    gains_wide = gains_full.astype(jnp.float32)
    shifts_wide = shifts_full.astype(jnp.float32)
    attn_norm, unit_a, inv_a = layer_norm(resid, gains_wide[0], shifts_wide[0])
    attn_in = attn_norm.astype(jnp.bfloat16)
    packed = jnp.dot(attn_in, qkv_full, preferred_element_type=jnp.float32)
    head_shape = (images, SEQ, HEADS, HEAD_DIM)
    query = (packed[:, :width] * HEAD_DIM ** (-0.5)).astype(jnp.bfloat16).reshape(head_shape)
    keyed = packed[:, width : 2 * width].astype(jnp.bfloat16).reshape(head_shape)
    valued = packed[:, 2 * width :].astype(jnp.bfloat16).reshape(head_shape)
    scores = jnp.einsum("iqhd,ikhd->ihqk", query, keyed, preferred_element_type=jnp.float32)
    probs, log_total = softmax_rows(scores)
    mixed = jnp.einsum(
        "ihqk,ikhd->iqhd", probs.astype(jnp.bfloat16), valued, preferred_element_type=jnp.float32
    )
    mixed = mixed.reshape(tok_count, width).astype(jnp.bfloat16)
    resid_mid = resid + jnp.dot(mixed, proj_full, preferred_element_type=jnp.float32)
    moe_norm, unit_b, inv_b = layer_norm(resid_mid, gains_wide[1], shifts_wide[1])
    moe_in = moe_norm.astype(jnp.bfloat16)
    logits = jnp.dot(moe_in, router_full, preferred_element_type=jnp.float32)
    router_probs, ignored_total = softmax_rows(logits)
    experts_total = router_full.shape[1]
    local_count = first_full.shape[0]
    peers = lax.axis_size("expert")
    capacity = max(2, 3 * tok_count // experts_total)
    route = routes[which].reshape(tok_count, 2)
    labels = jnp.arange(experts_total, dtype=jnp.int32)
    pick_first = (route[:, 0:1] == labels[None, :]).astype(jnp.int32)
    pick_second = (route[:, 1:2] == labels[None, :]).astype(jnp.int32)
    both_picks = pick_first + pick_second
    before = jnp.cumsum(both_picks, axis=0) - both_picks
    slot_first = route[:, 0] * capacity + jnp.sum(before * pick_first, axis=1)
    slot_second = route[:, 1] * capacity + jnp.sum(before * pick_second, axis=1)
    slot_ids = jnp.arange(experts_total * capacity, dtype=jnp.int32)
    place_first = (slot_ids[:, None] == slot_first[None, :]).astype(jnp.bfloat16)
    place_second = (slot_ids[:, None] == slot_second[None, :]).astype(jnp.bfloat16)
    outgoing = jnp.dot(place_first + place_second, moe_in, preferred_element_type=jnp.float32)
    outgoing = outgoing.astype(jnp.bfloat16).reshape(peers, local_count, capacity, width)
    incoming = lax.all_to_all(outgoing, "expert", split_axis=0, concat_axis=0, tiled=True)
    hidden_pre = jnp.einsum(
        "sjcd,jdf->sjcf", incoming, first_full, preferred_element_type=jnp.float32
    )
    hidden_act = gelu_value(hidden_pre).astype(jnp.bfloat16)
    result = jnp.einsum(
        "sjcf,jfd->sjcd", hidden_act, second_full, preferred_element_type=jnp.float32
    ).astype(jnp.bfloat16)
    returned = lax.all_to_all(result, "expert", split_axis=0, concat_axis=0, tiled=True).reshape(
        experts_total * capacity, width
    )
    pick_first_f = pick_first.astype(jnp.float32)
    pick_second_f = pick_second.astype(jnp.float32)
    gate_first = jnp.sum(router_probs * pick_first_f, axis=1)
    gate_second = jnp.sum(router_probs * pick_second_f, axis=1)
    back_first = jnp.take(returned, slot_first, axis=0).astype(jnp.float32)
    back_second = jnp.take(returned, slot_second, axis=0).astype(jnp.float32)
    resid_out = resid_mid + (gate_first[:, None] * back_first + gate_second[:, None] * back_second)
    saved = (
        qkv_full,
        proj_full,
        router_full,
        gains_wide,
        first_full,
        second_full,
        unit_a,
        inv_a,
        attn_in,
        query,
        keyed,
        valued,
        log_total,
        mixed,
        unit_b,
        inv_b,
        moe_in,
        router_probs,
        pick_first_f,
        pick_second_f,
        slot_first,
        slot_second,
        place_first,
        place_second,
        incoming,
        hidden_pre,
        hidden_act,
        returned,
        gate_first,
        gate_second,
    )
    return (resid_out, saved)


def layer_backward(grad_out, saved):
    (
        qkv_full,
        proj_full,
        router_full,
        gains_wide,
        first_full,
        second_full,
        unit_a,
        inv_a,
        attn_in,
        query,
        keyed,
        valued,
        log_total,
        mixed,
        unit_b,
        inv_b,
        moe_in,
        router_probs,
        pick_first_f,
        pick_second_f,
        slot_first,
        slot_second,
        place_first,
        place_second,
        incoming,
        hidden_pre,
        hidden_act,
        returned,
        gate_first,
        gate_second,
    ) = saved
    tok_count, width = grad_out.shape
    images = tok_count // SEQ
    back_first = jnp.take(returned, slot_first, axis=0).astype(jnp.float32)
    back_second = jnp.take(returned, slot_second, axis=0).astype(jnp.float32)
    grad_gate_first = jnp.sum(grad_out * back_first, axis=1)
    grad_gate_second = jnp.sum(grad_out * back_second, axis=1)
    send_first = (gate_first[:, None] * grad_out).astype(jnp.bfloat16)
    send_second = (gate_second[:, None] * grad_out).astype(jnp.bfloat16)
    slot_grads = jnp.dot(place_first, send_first, preferred_element_type=jnp.float32) + jnp.dot(
        place_second, send_second, preferred_element_type=jnp.float32
    )
    slot_grads = slot_grads.astype(jnp.bfloat16).reshape(incoming.shape)
    grad_result = lax.all_to_all(slot_grads, "expert", split_axis=0, concat_axis=0, tiled=True)
    grad_act = jnp.einsum(
        "sjcd,jfd->sjcf", grad_result, second_full, preferred_element_type=jnp.float32
    )
    grad_second = jnp.einsum(
        "sjcf,sjcd->jfd", hidden_act, grad_result, preferred_element_type=jnp.float32
    )
    grad_pre = (grad_act * gelu_slope(hidden_pre)).astype(jnp.bfloat16)
    grad_first = jnp.einsum(
        "sjcd,sjcf->jdf", incoming, grad_pre, preferred_element_type=jnp.float32
    )
    grad_rows = jnp.einsum(
        "sjcf,jdf->sjcd", grad_pre, first_full, preferred_element_type=jnp.float32
    ).astype(jnp.bfloat16)
    grad_back = lax.all_to_all(
        grad_rows, "expert", split_axis=0, concat_axis=0, tiled=True
    ).reshape(-1, width)
    grad_moe = jnp.einsum(
        "st,sd->td", place_first + place_second, grad_back, preferred_element_type=jnp.float32
    )
    grad_probs = pick_first_f * grad_gate_first[:, None] + pick_second_f * grad_gate_second[:, None]
    weighted = jnp.sum(router_probs * grad_probs, axis=1, keepdims=True)
    grad_logits = (router_probs * (grad_probs - weighted)).astype(jnp.bfloat16)
    grad_router = jnp.einsum("td,te->de", moe_in, grad_logits, preferred_element_type=jnp.float32)
    grad_moe = grad_moe + jnp.einsum(
        "te,de->td", grad_logits, router_full, preferred_element_type=jnp.float32
    )
    grad_norm_b, gain_b_grad, shift_b_grad = norm_back(grad_moe, unit_b, inv_b, gains_wide[1])
    grad_mid = grad_out + grad_norm_b
    grad_branch = grad_mid.astype(jnp.bfloat16)
    grad_proj = jnp.einsum("td,te->de", mixed, grad_branch, preferred_element_type=jnp.float32)
    grad_mixed = jnp.einsum("te,de->td", grad_branch, proj_full, preferred_element_type=jnp.float32)
    grad_mixed = grad_mixed.astype(jnp.bfloat16).reshape(images, SEQ, HEADS, HEAD_DIM)
    scores = jnp.einsum("iqhd,ikhd->ihqk", query, keyed, preferred_element_type=jnp.float32)
    probs = jnp.exp(scores - log_total)
    grad_weights = jnp.einsum(
        "iqhd,ikhd->ihqk", grad_mixed, valued, preferred_element_type=jnp.float32
    )
    grad_valued = jnp.einsum(
        "ihqk,iqhd->ikhd",
        probs.astype(jnp.bfloat16),
        grad_mixed,
        preferred_element_type=jnp.float32,
    ).astype(jnp.bfloat16)
    row_inner = jnp.sum(probs * grad_weights, axis=-1, keepdims=True)
    grad_scores = (probs * (grad_weights - row_inner)).astype(jnp.bfloat16)
    grad_query = jnp.einsum(
        "ihqk,ikhd->iqhd", grad_scores, keyed, preferred_element_type=jnp.float32
    ).astype(jnp.bfloat16)
    grad_query = grad_query * jnp.asarray(HEAD_DIM ** (-0.5), jnp.bfloat16)
    grad_keyed = jnp.einsum(
        "ihqk,iqhd->ikhd", grad_scores, query, preferred_element_type=jnp.float32
    ).astype(jnp.bfloat16)
    grad_packed = jnp.concatenate(
        [
            grad_query.reshape(tok_count, width),
            grad_keyed.reshape(tok_count, width),
            grad_valued.reshape(tok_count, width),
        ],
        axis=1,
    )
    grad_qkv = jnp.einsum("td,te->de", attn_in, grad_packed, preferred_element_type=jnp.float32)
    grad_attn = jnp.einsum("te,de->td", grad_packed, qkv_full, preferred_element_type=jnp.float32)
    grad_norm_a, gain_a_grad, shift_a_grad = norm_back(grad_attn, unit_a, inv_a, gains_wide[0])
    grad_in = grad_mid + grad_norm_a
    dense = (
        grad_qkv,
        grad_proj,
        grad_router,
        jnp.stack([gain_a_grad, gain_b_grad]),
        jnp.stack([shift_a_grad, shift_b_grad]),
    )
    return (grad_in, dense, (grad_first, grad_second))


def body(
    embedded, cotangent, w_qkv, w_proj, w_router, norm_gains, norm_shifts, w_first, w_second, routes
):
    images, length, width = embedded.shape
    tok_count = images * length
    resid = embedded.reshape(tok_count, width).astype(jnp.float32)
    layer_inputs = []
    for which in range(LAYERS):
        layer_inputs.append(resid)
        resid, saved = layer_forward(
            resid,
            which,
            w_qkv,
            w_proj,
            w_router,
            norm_gains,
            norm_shifts,
            w_first,
            w_second,
            routes,
        )
    out_images = resid.reshape(images, length, width).astype(jnp.bfloat16)
    grad = cotangent.reshape(tok_count, width).astype(jnp.float32)
    dense_layers = []
    expert_layers = []
    for which in reversed(range(LAYERS)):
        ignored, saved = layer_forward(
            layer_inputs[which],
            which,
            w_qkv,
            w_proj,
            w_router,
            norm_gains,
            norm_shifts,
            w_first,
            w_second,
            routes,
        )
        grad, dense, expert_part = layer_backward(grad, saved)
        totals = (
            lax.psum(dense[0].astype(jnp.bfloat16), "expert").astype(jnp.float32),
            lax.psum(dense[1].astype(jnp.bfloat16), "expert").astype(jnp.float32),
            lax.psum(dense[2].astype(jnp.bfloat16), "expert").astype(jnp.float32),
            lax.psum(dense[3].astype(jnp.bfloat16), "expert").astype(jnp.float32),
            lax.psum(dense[4].astype(jnp.bfloat16), "expert").astype(jnp.float32),
        )
        shares = (
            lax.psum_scatter(
                totals[0].astype(jnp.bfloat16), "dp", scatter_dimension=0, tiled=True
            ).astype(jnp.float32),
            lax.psum_scatter(
                totals[1].astype(jnp.bfloat16), "dp", scatter_dimension=0, tiled=True
            ).astype(jnp.float32),
            lax.psum_scatter(
                totals[2].astype(jnp.bfloat16), "dp", scatter_dimension=0, tiled=True
            ).astype(jnp.float32),
            lax.psum_scatter(
                totals[3].astype(jnp.bfloat16), "dp", scatter_dimension=1, tiled=True
            ).astype(jnp.float32),
            lax.psum_scatter(
                totals[4].astype(jnp.bfloat16), "dp", scatter_dimension=1, tiled=True
            ).astype(jnp.float32),
        )
        expert_shares = (
            lax.psum_scatter(
                expert_part[0].astype(jnp.bfloat16), "dp", scatter_dimension=2, tiled=True
            ).astype(jnp.float32),
            lax.psum_scatter(
                expert_part[1].astype(jnp.bfloat16), "dp", scatter_dimension=1, tiled=True
            ).astype(jnp.float32),
        )
        dense_layers.insert(0, shares)
        expert_layers.insert(0, expert_shares)
    grad_images = grad.reshape(images, length, width)
    grad_qkv = jnp.stack([entry[0] for entry in dense_layers])
    grad_proj = jnp.stack([entry[1] for entry in dense_layers])
    grad_router = jnp.stack([entry[2] for entry in dense_layers])
    grad_gains = jnp.stack([entry[3] for entry in dense_layers])
    grad_shifts = jnp.stack([entry[4] for entry in dense_layers])
    grad_first = jnp.stack([entry[0] for entry in expert_layers])
    grad_second = jnp.stack([entry[1] for entry in expert_layers])
    return (
        out_images,
        grad_images,
        grad_qkv,
        grad_proj,
        grad_router,
        grad_gains,
        grad_shifts,
        grad_first,
        grad_second,
    )


def solution(mesh):
    return jax.shard_map(
        body,
        mesh=mesh,
        in_specs=(
            P(("dp", "expert"), None, None),
            P(("dp", "expert"), None, None),
            P(None, "dp", None),
            P(None, "dp", None),
            P(None, "dp", None),
            P(None, None, "dp"),
            P(None, None, "dp"),
            P(None, "expert", None, "dp"),
            P(None, "expert", "dp", None),
            P(None, ("dp", "expert"), None, None),
        ),
        out_specs=(
            P(("dp", "expert"), None, None),
            P(("dp", "expert"), None, None),
            P(None, "dp", None),
            P(None, "dp", None),
            P(None, "dp", None),
            P(None, None, "dp"),
            P(None, None, "dp"),
            P(None, "expert", None, "dp"),
            P(None, "expert", "dp", None),
        ),
        check_vma=False,
    )
```

profile of v0, /device:TPU:0, one launch (start us, length us, event | category | flops | bytes accessed | tf_op | source)
XLA Modules:
  0.0 1092.9 jit_solution(856967177096205174)
XLA Ops:
  16.5 17.0 %all-gather = bf16[1,2,512]{1,0,2:T(2,128)(2,1)S(1)} all-gather(bf16[1,2,64]{1,0,2:T(2,128)(2,1)S(1)} %copy.377), channel_id=2, replica_groups=mesh['dp'=8,'expert'=4] {'dp'}, dimensions={2}, use_global_device_ids=true | all-gather | bytes 2304 | tf_op jit(solution)/shard_map/all_gather | solution.py:56
  37.7 14.6 %all-gather.1 = bf16[1,2,512]{1,0,2:T(2,128)(2,1)S(1)} all-gather(bf16[1,2,64]{1,0,2:T(2,128)(2,1)S(1)} %copy.378), channel_id=3, replica_groups=mesh['dp'=8,'expert'=4] {'dp'}, dimensions={2}, use_global_device_ids=true | all-gather | bytes 2304 | tf_op jit(solution)/shard_map/all_gather | solution.py:57
  55.9 25.2 %all-gather.3 = bf16[1,512,512]{2,1,0:T(8,128)(2,1)} all-gather(bf16[1,64,512]{2,1,0:T(8,128)(2,1)S(1)} %get-tuple-element.126), channel_id=5, replica_groups=mesh['dp'=8,'expert'=4] {'dp'}, dimensions={1}, use_global_device_ids=true | all-gather | bytes 589824 | tf_op jit(solution)/shard_map/all_gather | solution.py:54
  122.9 15.7 %all-gather.4 = bf16[1,512,8]{2,0,1:T(2,128)(2,1)S(1)} all-gather(bf16[1,64,8]{2,0,1:T(2,128)(2,1)} %copy.379), channel_id=6, replica_groups=mesh['dp'=8,'expert'=4] {'dp'}, dimensions={1}, use_global_device_ids=true | all-gather | bytes 9216 | tf_op jit(solution)/shard_map/all_gather | solution.py:55
  140.0 14.2 %all-gather.7 = bf16[1,2,512]{1,0,2:T(2,128)(2,1)S(1)} all-gather(bf16[1,2,64]{1,0,2:T(2,128)(2,1)S(1)} %copy.380), channel_id=9, replica_groups=mesh['dp'=8,'expert'=4] {'dp'}, dimensions={2}, use_global_device_ids=true | all-gather | bytes 2304 | tf_op jit(solution)/shard_map/all_gather | solution.py:56
  155.8 15.6 %all-gather.8 = bf16[1,2,512]{1,0,2:T(2,128)(2,1)S(1)} all-gather(bf16[1,2,64]{1,0,2:T(2,128)(2,1)} %copy.381), channel_id=10, replica_groups=mesh['dp'=8,'expert'=4] {'dp'}, dimensions={2}, use_global_device_ids=true | all-gather | bytes 2304 | tf_op jit(solution)/shard_map/all_gather | solution.py:57
  206.3 17.5 %all-gather.10 = bf16[1,512,512]{2,1,0:T(8,128)(2,1)} all-gather(bf16[1,64,512]{2,1,0:T(8,128)(2,1)S(1)} %copy-done.50), channel_id=12, replica_groups=mesh['dp'=8,'expert'=4] {'dp'}, dimensions={1}, use_global_device_ids=true | all-gather | bytes 589824 | tf_op jit(solution)/shard_map/all_gather | solution.py:54
  287.3 14.8 %all-gather.11 = bf16[1,512,8]{2,0,1:T(2,128)(2,1)S(1)} all-gather(bf16[1,64,8]{2,0,1:T(2,128)(2,1)} %copy.382), channel_id=13, replica_groups=mesh['dp'=8,'expert'=4] {'dp'}, dimensions={1}, use_global_device_ids=true | all-gather | bytes 9216 | tf_op jit(solution)/shard_map/all_gather | solution.py:55
  330.4 15.1 %all-to-all-done.3 = bf16[4,2,147,512]{3,1,2,0:T(2,128)(2,1)} async-done(((bf16[4,2,147,512]{3,1,2,0:T(2,128)(2,1)}), bf16[4,2,147,512]{3,1,2,0:T(2,128)(2,1)}, u32[]{:S(2)}, u32[]{:S(2)}) %all-to-all-start.3) | async-done | bytes 1204256 | tf_op jit(solution)/shard_map/all_to_all | solution.py:110
  369.8 18.9 %all_to_all.44 = bf16[4,2,147,512]{3,1,2,0:T(2,128)(2,1)S(1)} all-to-all(bf16[4,2,147,512]{3,1,2,0:T(2,128)(2,1)S(1)} %copy.295), channel_id=1, replica_groups=mesh['dp'=8,'expert'=4] {'expert'}, dimensions={0} | all-to-all | bytes 2408448 | tf_op jit(solution)/shard_map/all_to_all | solution.py:200
  406.2 14.4 %all-to-all-done.5 = bf16[4,2,147,512]{3,1,2,0:T(2,128)(2,1)} async-done(((bf16[4,2,147,512]{3,1,2,0:T(2,128)(2,1)}), bf16[4,2,147,512]{3,1,2,0:T(2,128)(2,1)}, u32[]{:S(2)}, u32[]{:S(2)}) %all-to-all-start.5) | async-done | bytes 1204256 | tf_op jit(solution)/shard_map/all_to_all | solution.py:214
  471.1 18.4 %all_to_all.45 = bf16[4,2,147,512]{3,1,2,0:T(2,128)(2,1)S(1)} all-to-all(bf16[4,2,147,512]{3,1,2,0:T(2,128)(2,1)S(1)} %copy.311), channel_id=1, replica_groups=mesh['dp'=8,'expert'=4] {'expert'}, dimensions={0} | all-to-all | bytes 2408448 | tf_op jit(solution)/shard_map/all_to_all | solution.py:200
  574.3 35.1 %reduce-scatter.37.cloned.1.call-done = bf16[64,1536]{1,0:T(8,128)(2,1)} async-done(((bf16[512,1536]{1,0:T(8,128)(2,1)}), bf16[64,1536]{1,0:T(8,128)(2,1)}) %reduce-scatter.37.cloned.1.call-update) | async-done | bytes 196624 | tf_op jit(solution)/shard_map/reduce_scatter | solution.py:322
  609.4 34.7 %reduce-scatter.35.cloned.1.call-done = bf16[64,1536]{1,0:T(8,128)(2,1)} async-done(((bf16[512,1536]{1,0:T(8,128)(2,1)}), bf16[64,1536]{1,0:T(8,128)(2,1)}) %reduce-scatter.35.cloned.1.call-update) | async-done | bytes 196624 | tf_op jit(solution)/shard_map/reduce_scatter | solution.py:322
  681.8 25.0 %reduce-scatter.53.cloned.1.call-done = bf16[64,2]{1,0:T(8,128)(2,1)} async-done(((bf16[512,2]{1,0:T(8,128)(2,1)}), bf16[64,2]{1,0:T(8,128)(2,1)}) %reduce-scatter.53.cloned.1.call-update) | async-done | bytes 272
  707.6 30.8 %reduce-scatter.49.cloned.1.call-done = bf16[64,2]{1,0:T(8,128)(2,1)} async-done(((bf16[512,2]{1,0:T(8,128)(2,1)}), bf16[64,2]{1,0:T(8,128)(2,1)}) %reduce-scatter.49.cloned.1.call-update) | async-done | bytes 272
  739.2 30.7 %reduce-scatter.43.cloned.1.call-done = bf16[64,8]{1,0:T(8,128)(2,1)} async-done(((bf16[512,8]{1,0:T(8,128)(2,1)}), bf16[64,8]{1,0:T(8,128)(2,1)}) %reduce-scatter.43.cloned.1.call-update) | async-done | bytes 1040
  772.6 28.1 %reduce-scatter.51.cloned.1.call-done = bf16[64,2]{1,0:T(8,128)(2,1)} async-done(((bf16[512,2]{1,0:T(8,128)(2,1)}), bf16[64,2]{1,0:T(8,128)(2,1)}) %reduce-scatter.51.cloned.1.call-update) | async-done | bytes 272
  801.5 30.6 %reduce-scatter.47.cloned.1.call-done = bf16[64,2]{1,0:T(8,128)(2,1)} async-done(((bf16[512,2]{1,0:T(8,128)(2,1)}), bf16[64,2]{1,0:T(8,128)(2,1)}) %reduce-scatter.47.cloned.1.call-update) | async-done | bytes 272
  844.7 34.3 %all-reduce.6.cloned.1.call-done = (bf16[64,1536]{1,0:T(8,128)(2,1)}, bf16[64,1536]{1,0:T(8,128)(2,1)}, bf16[64,512]{1,0:T(8,128)(2,1)}, bf16[64,512]{1,0:T(8,128)(2,1)}) async-done(((bf16[64,1536]{1,0:T(8,128)(2,1)}, bf16[64,1536]{1,0:T(8,128)(2,1)}, bf16[64,512]{1,0:T(8,128)(2,1)}, bf16[64,512]{1,0:T(8,128)(2,1)}), (bf16[64,1536]{1,0:T(8,128)(2,1)}, bf16[64,1536]{1,0:T(8,128)(2,1)}, ...) | async-done | bytes 524304 | tf_op jit(solution)/shard_map/psum | solution.py:315
  882.6 48.5 %reduce-scatter.33.cloned.1.call-done = bf16[2,256,512]{2,1,0:T(8,128)(2,1)} async-done(((bf16[2,2048,512]{2,1,0:T(8,128)(2,1)}), bf16[2,256,512]{2,1,0:T(8,128)(2,1)}) %reduce-scatter.33.cloned.1.call-update) | async-done | bytes 524304 | tf_op jit(solution)/shard_map/reduce_scatter | solution.py:342
  931.1 50.7 %reduce-scatter.31.cloned.1.call-done = bf16[2,256,512]{2,1,0:T(8,128)(2,1)} async-done(((bf16[2,2048,512]{2,1,0:T(8,128)(2,1)}), bf16[2,256,512]{2,1,0:T(8,128)(2,1)}) %reduce-scatter.31.cloned.1.call-update) | async-done | bytes 524304 | tf_op jit(solution)/shard_map/reduce_scatter | solution.py:342
  984.5 47.9 %reduce-scatter.29.cloned.1.call-done = bf16[2,512,256]{2,1,0:T(8,128)(2,1)} async-done(((bf16[2,512,2048]{2,1,0:T(8,128)(2,1)}), bf16[2,512,256]{2,1,0:T(8,128)(2,1)}) %reduce-scatter.29.cloned.1.call-update) | async-done | bytes 524304 | tf_op jit(solution)/shard_map/reduce_scatter | solution.py:339
  1032.4 50.7 %reduce-scatter.27.cloned.1.call-done = bf16[2,512,256]{2,1,0:T(8,128)(2,1)} async-done(((bf16[2,512,2048]{2,1,0:T(8,128)(2,1)}), bf16[2,512,256]{2,1,0:T(8,128)(2,1)}) %reduce-scatter.27.cloned.1.call-update) | async-done | bytes 524304 | tf_op jit(solution)/shard_map/reduce_scatter | solution.py:339
  (595 shorter events, 427.7 us)
Async XLA Ops:
  7.2 80.8 %all-gather.21.cloned.1.call-start = ((), (), s32[]{:S(2)}) async-start(), calls=%async_computation.26 | async-start | bytes 1769472 | tf_op jit(solution)/shard_map/all_gather | solution.py:53
  9.1 174.3 %all-gather.23.cloned.1.call-start = ((), (), s32[]{:S(2)}) async-start(), calls=%async_computation.27 | async-start | bytes 4718592 | tf_op jit(solution)/shard_map/all_gather | solution.py:60
  11.5 181.1 %all-gather.25.cloned.1.call-start = ((), (), s32[]{:S(2)}) async-start(), calls=%async_computation.28 | async-start | bytes 4718592 | tf_op jit(solution)/shard_map/all_gather | solution.py:61
  12.6 229.4 %all-gather.27.cloned.1.call-start = ((), (), s32[]{:S(2)}) async-start(), calls=%async_computation.29 | async-start | bytes 1769472 | tf_op jit(solution)/shard_map/all_gather | solution.py:53
  13.2 293.7 %all-gather.29.cloned.1.call-start = ((), (), s32[]{:S(2)}) async-start(), calls=%async_computation.30 | async-start | bytes 4718592 | tf_op jit(solution)/shard_map/all_gather | solution.py:60
  13.8 302.3 %all-gather.31.cloned.1.call-start = ((), (), s32[]{:S(2)}) async-start(), calls=%async_computation.31 | async-start | bytes 4718592 | tf_op jit(solution)/shard_map/all_gather | solution.py:61
  118.6 64.8 %all-to-all-start = ((bf16[4,2,147,512]{3,1,2,0:T(2,128)(2,1)}), bf16[4,2,147,512]{3,1,2,0:T(2,128)(2,1)}, u32[]{:S(2)}, u32[]{:S(2)}) async-start(bf16[4,2,147,512]{3,1,2,0:T(2,128)(2,1)} %copy.273), calls=%async_computation | async-start | bytes 2408448 | tf_op jit(solution)/shard_map/all_to_all | solution.py:102
  201.4 23.8 %all-to-all-start.1 = ((bf16[4,2,147,512]{3,1,2,0:T(2,128)(2,1)}), bf16[4,2,147,512]{3,1,2,0:T(2,128)(2,1)}, u32[]{:S(2)}, u32[]{:S(2)}) async-start(bf16[4,2,147,512]{3,1,2,0:T(2,128)(2,1)} %copy.275), calls=%async_computation.1 | async-start | bytes 2408448 | tf_op jit(solution)/shard_map/all_to_all | solution.py:110
  282.2 24.7 %all-to-all-start.2 = ((bf16[4,2,147,512]{3,1,2,0:T(2,128)(2,1)}), bf16[4,2,147,512]{3,1,2,0:T(2,128)(2,1)}, u32[]{:S(2)}, u32[]{:S(2)}) async-start(bf16[4,2,147,512]{3,1,2,0:T(2,128)(2,1)} %copy.290), calls=%async_computation.2 | async-start | bytes 2408448 | tf_op jit(solution)/shard_map/all_to_all | solution.py:102
  507.1 62.2 %reduce-scatter.41.cloned.1.call-start = ((), (), s32[]{:S(2)}) async-start(), calls=%async_computation.35 | async-start | bytes 589824 | tf_op jit(solution)/shard_map/reduce_scatter | solution.py:325
  509.7 64.6 %reduce-scatter.39.cloned.1.call-start = ((), (), s32[]{:S(2)}) async-start(), calls=%async_computation.34 | async-start | bytes 589824 | tf_op jit(solution)/shard_map/reduce_scatter | solution.py:325
  532.0 77.4 %reduce-scatter.37.cloned.1.call-start = ((), (), s32[]{:S(2)}) async-start(), calls=%async_computation.33 | async-start | bytes 1769472 | tf_op jit(solution)/shard_map/reduce_scatter | solution.py:322
  536.1 108.0 %reduce-scatter.35.cloned.1.call-start = ((), (), s32[]{:S(2)}) async-start(), calls=%async_computation.32 | async-start | bytes 1769472 | tf_op jit(solution)/shard_map/reduce_scatter | solution.py:322
  560.0 119.7 %reduce-scatter.45.cloned.1.call-start = ((), (), s32[]{:S(2)}) async-start(), calls=%async_computation.37 | async-start | bytes 147456
  561.0 145.8 %reduce-scatter.53.cloned.1.call-start = ((), (), s32[]{:S(2)}) async-start(), calls=%async_computation.41 | async-start | bytes 147456
  561.9 176.5 %reduce-scatter.49.cloned.1.call-start = ((), (), s32[]{:S(2)}) async-start(), calls=%async_computation.39 | async-start | bytes 147456
  562.9 207.0 %reduce-scatter.43.cloned.1.call-start = ((), (), s32[]{:S(2)}) async-start(), calls=%async_computation.36 | async-start | bytes 147456
  563.9 236.8 %reduce-scatter.51.cloned.1.call-start = ((), (), s32[]{:S(2)}) async-start(), calls=%async_computation.40 | async-start | bytes 147456
  568.2 263.8 %reduce-scatter.47.cloned.1.call-start = ((), (), s32[]{:S(2)}) async-start(), calls=%async_computation.38 | async-start | bytes 147456
  569.1 309.9 %all-reduce.6.cloned.1.call-start = ((), (), s32[]{:S(2)}) async-start(), calls=%async_computation.42 | async-start | bytes 1048576 | tf_op jit(solution)/shard_map/psum | solution.py:315
  644.1 287.0 %reduce-scatter.33.cloned.1.call-start = ((), (), s32[]{:S(2)}) async-start(), calls=%async_computation.25 | async-start | bytes 4718592 | tf_op jit(solution)/shard_map/reduce_scatter | solution.py:342
  652.8 329.1 %reduce-scatter.31.cloned.1.call-start = ((), (), s32[]{:S(2)}) async-start(), calls=%async_computation.24 | async-start | bytes 4718592 | tf_op jit(solution)/shard_map/reduce_scatter | solution.py:342
  662.6 369.8 %reduce-scatter.29.cloned.1.call-start = ((), (), s32[]{:S(2)}) async-start(), calls=%async_computation.23 | async-start | bytes 4718592 | tf_op jit(solution)/shard_map/reduce_scatter | solution.py:339
  671.0 412.1 %reduce-scatter.27.cloned.1.call-start = ((), (), s32[]{:S(2)}) async-start(), calls=%async_computation.22 | async-start | bytes 4718592 | tf_op jit(solution)/shard_map/reduce_scatter | solution.py:339
  (142 other events, 1518.4 us)
Sparse Core Ops, SparseCore 0:
  10.2 29.4 all-gather.20
  41.3 51.4 all-gather.22
  94.4 47.3 all-gather.24
  143.9 25.8 all-gather.26
  171.2 49.7 all-gather.28
  222.4 45.8 all-gather.30
  510.1 32.3 reduce-scatter.40
  544.8 29.4 reduce-scatter.38
  577.2 32.1 reduce-scatter.36
  611.6 32.4 reduce-scatter.34
  646.9 28.9 reduce-scatter.44
  678.1 28.7 reduce-scatter.52
  709.6 28.7 reduce-scatter.48
  741.1 28.7 reduce-scatter.42
  771.9 28.7 reduce-scatter.50
  803.4 28.6 reduce-scatter.46
  835.2 43.8 all-reduce.5
  881.2 49.8 reduce-scatter.32
  933.4 48.3 reduce-scatter.30
  984.0 48.3 reduce-scatter.28
  1034.7 48.3 reduce-scatter.26
where the time goes:
time: 1100 us; the launch traced here: 1090 us
  waiting for transfers between devices  495 us (45%)
  local copies, waits for them, and re-layouts  186 us (17%)
  blocking collectives  182 us (17%)
  matrix products  151 us (14%)
  other arithmetic  35 us (3%)
  starting transfers between devices  27.2 us (2%)
  between operations  16.6 us (2%)
    unnamed x27, waiting for transfers between devices  147 us
    reduce_scatter x2, waiting for transfers between devices, body(): lax.psum_scatter(expert_part[1].astype(jnp.bfloat16), 'dp', scatter_dimen...  99.3 us
    reduce_scatter x2, waiting for transfers between devices, body(): lax.psum_scatter(expert_part[0].astype(jnp.bfloat16), 'dp', scatter_dimen...  98.6 us
    reduce_scatter x2, waiting for transfers between devices, body(): lax.psum_scatter(totals[0].astype(jnp.bfloat16), 'dp', scatter_dimension=...  69.8 us
    all_gather x2, blocking collectives, layer_forward(): lax.all_gather(w_proj[which], 'dp', axis=0, tiled=True)  42.8 us
    all_to_all x2, blocking collectives, layer_backward(): lax.all_to_all(slot_grads, 'expert', split_axis=0, concat_axis=0, tiled=T...  37.3 us
    psum x1, waiting for transfers between devices, body(): lax.psum(dense[0].astype(jnp.bfloat16), 'expert').astype(jnp.float32)  34.3 us
    unnamed x304, local copies, waits for them, and re-layouts  32.4 us
  transfers between devices with their start and end apart: 27, of which 16 were waited for; matrix products, arithmetic and copies ran while one was open for 23% of the time, Pallas kernels for 0%

commit v1 on v0

--- a/solution.py
+++ b/solution.py
@@ -12,6 +12,28 @@
 INV_ROOT_TAU = 0.3989422804014327
 
 
+def laid_out(blocks, dim):
+    shape = list(blocks.shape[1:])
+    shape[dim] *= blocks.shape[0]
+    return jnp.moveaxis(blocks, 0, dim).reshape(shape)
+
+
+def doubled(x, axis):
+    size = lax.axis_size(axis)
+    blocks = x[None]
+    for level in range(size.bit_length() - 1):
+        stride = 1 << level
+        partner_block = lax.ppermute(blocks, axis, [(i, i ^ stride) for i in range(size)])
+        both = jnp.stack([blocks, partner_block])
+        upper = lax.axis_index(axis) >> level & 1
+        blocks = jnp.where(upper == 0, both, both[::-1]).reshape(-1, *x.shape)
+    return blocks
+
+
+def collect(x, axis, dim):
+    return laid_out(doubled(x, axis), dim)
+
+
 def layer_norm(values, scale_in, shift_in):
     center = values - jnp.mean(values, axis=-1, keepdims=True)
     variance = jnp.mean(center * center, axis=-1, keepdims=True)
@@ -51,7 +73,7 @@
 ):
     qkv_full, proj_full, router_full, gains_full, shifts_full = (
         lax.all_gather(w_qkv[which], "dp", axis=0, tiled=True),
-        lax.all_gather(w_proj[which], "dp", axis=0, tiled=True),
+        collect(w_proj[which], "dp", 0),
         lax.all_gather(w_router[which], "dp", axis=0, tiled=True),
         lax.all_gather(norm_gains[which], "dp", axis=1, tiled=True),
         lax.all_gather(norm_shifts[which], "dp", axis=1, tiled=True),

time: 1100 us -> 1100 us (level)
  blocking collectives: 182 us -> 155 us
  waiting for transfers between devices: 495 us -> 509 us
    all_gather x2 -> x0, blocking collectives: 42.8 us -> none  [layer_forward(): lax.all_gather(w_proj[which], 'dp', axis=0, tiled=True)]
    ppermute x0 -> x6, waiting for transfers between devices: none -> 11.1 us  [doubled(): lax.ppermute(blocks, axis, [(i, i ^ stride) for i in range(size)])]
    unnamed x304 -> x310, local copies, waits for them, and re-layouts: 32.4 us -> 30.6 us
  transfers between devices with their start and end apart: 27 -> 33, of which waited for: 16 -> 19; matrix products, arithmetic and copies ran while one was open for 23% -> 23% of each run, Pallas kernels for 0% -> 0%
where the time goes in v1:
time: 1100 us; the launch traced here: 1090 us
  waiting for transfers between devices  509 us (46%)
  local copies, waits for them, and re-layouts  183 us (17%)
  blocking collectives  155 us (14%)
  matrix products  151 us (14%)
  other arithmetic  38.4 us (3%)
  starting transfers between devices  34.7 us (3%)
  between operations  16.7 us (2%)
    unnamed x27, waiting for transfers between devices  147 us
    reduce_scatter x2, waiting for transfers between devices, body(): lax.psum_scatter(expert_part[1].astype(jnp.bfloat16), 'dp', scatter_dimen...  99.3 us
    reduce_scatter x2, waiting for transfers between devices, body(): lax.psum_scatter(expert_part[0].astype(jnp.bfloat16), 'dp', scatter_dimen...  98.6 us
    reduce_scatter x2, waiting for transfers between devices, body(): lax.psum_scatter(totals[0].astype(jnp.bfloat16), 'dp', scatter_dimension=...  70.1 us
    all_gather x2, blocking collectives, layer_forward(): lax.all_gather(norm_gains[which], 'dp', axis=1, tiled=True)  40.4 us
    all_to_all x2, blocking collectives, layer_backward(): lax.all_to_all(slot_grads, 'expert', split_axis=0, concat_axis=0, tiled=T...  36.9 us
    all_gather x2, blocking collectives, layer_forward(): lax.all_gather(norm_shifts[which], 'dp', axis=1, tiled=True)  35.8 us
    psum x1, waiting for transfers between devices, body(): lax.psum(dense[0].astype(jnp.bfloat16), 'expert').astype(jnp.float32)  34.4 us
  transfers between devices with their start and end apart: 33, of which 19 were waited for; matrix products, arithmetic and copies ran while one was open for 23% of the time, Pallas kernels for 0%

profile of v1, /device:TPU:0, one launch (start us, length us, event | category | flops | bytes accessed | tf_op | source)
XLA Modules:
  0.0 1086.9 jit_solution(1104849088516114280)
XLA Ops:
  15.2 16.9 %all-gather = bf16[1,2,512]{1,0,2:T(2,128)(2,1)S(1)} all-gather(bf16[1,2,64]{1,0,2:T(2,128)(2,1)S(1)} %copy.387), channel_id=2, replica_groups=mesh['dp'=8,'expert'=4] {'dp'}, dimensions={2}, use_global_device_ids=true | all-gather | bytes 2304 | tf_op jit(solution)/shard_map/all_gather | solution.py:78
  42.8 15.4 %all-gather.1 = bf16[1,2,512]{1,0,2:T(2,128)(2,1)S(1)} all-gather(bf16[1,2,64]{1,0,2:T(2,128)(2,1)S(1)} %copy.388), channel_id=3, replica_groups=mesh['dp'=8,'expert'=4] {'dp'}, dimensions={2}, use_global_device_ids=true | all-gather | bytes 2304 | tf_op jit(solution)/shard_map/all_gather | solution.py:79
  58.6 23.5 %all-gather.6 = bf16[1,2,512]{1,0,2:T(2,128)(2,1)S(1)} all-gather(bf16[1,2,64]{1,0,2:T(2,128)(2,1)S(1)} %copy.390), channel_id=8, replica_groups=mesh['dp'=8,'expert'=4] {'dp'}, dimensions={2}, use_global_device_ids=true | all-gather | bytes 2304 | tf_op jit(solution)/shard_map/all_gather | solution.py:78
  98.5 20.4 %all-gather.7 = bf16[1,2,512]{1,0,2:T(2,128)(2,1)S(1)} all-gather(bf16[1,2,64]{1,0,2:T(2,128)(2,1)S(1)} %copy.391), channel_id=9, replica_groups=mesh['dp'=8,'expert'=4] {'dp'}, dimensions={2}, use_global_device_ids=true | all-gather | bytes 2304 | tf_op jit(solution)/shard_map/all_gather | solution.py:79
  161.8 17.3 %all-gather.3 = bf16[1,512,8]{2,0,1:T(2,128)(2,1)S(1)} all-gather(bf16[1,64,8]{2,0,1:T(2,128)(2,1)} %copy.389), channel_id=5, replica_groups=mesh['dp'=8,'expert'=4] {'dp'}, dimensions={1}, use_global_device_ids=true | all-gather | bytes 9216 | tf_op jit(solution)/shard_map/all_gather | solution.py:77
  282.5 14.5 %all-gather.9 = bf16[1,512,8]{2,0,1:T(2,128)(2,1)S(1)} all-gather(bf16[1,64,8]{2,0,1:T(2,128)(2,1)} %copy.392), channel_id=11, replica_groups=mesh['dp'=8,'expert'=4] {'dp'}, dimensions={1}, use_global_device_ids=true | all-gather | bytes 9216 | tf_op jit(solution)/shard_map/all_gather | solution.py:77
  325.6 15.0 %all-to-all-done.3 = bf16[4,2,147,512]{3,1,2,0:T(2,128)(2,1)} async-done(((bf16[4,2,147,512]{3,1,2,0:T(2,128)(2,1)}), bf16[4,2,147,512]{3,1,2,0:T(2,128)(2,1)}, u32[]{:S(2)}, u32[]{:S(2)}) %all-to-all-start.3) | async-done | bytes 1204256 | tf_op jit(solution)/shard_map/all_to_all | solution.py:132
  364.9 18.6 %all_to_all.44 = bf16[4,2,147,512]{3,1,2,0:T(2,128)(2,1)S(1)} all-to-all(bf16[4,2,147,512]{3,1,2,0:T(2,128)(2,1)S(1)} %copy.305), channel_id=1, replica_groups=mesh['dp'=8,'expert'=4] {'expert'}, dimensions={0} | all-to-all | bytes 2408448 | tf_op jit(solution)/shard_map/all_to_all | solution.py:222
  401.2 14.4 %all-to-all-done.5 = bf16[4,2,147,512]{3,1,2,0:T(2,128)(2,1)} async-done(((bf16[4,2,147,512]{3,1,2,0:T(2,128)(2,1)}), bf16[4,2,147,512]{3,1,2,0:T(2,128)(2,1)}, u32[]{:S(2)}, u32[]{:S(2)}) %all-to-all-start.5) | async-done | bytes 1204256 | tf_op jit(solution)/shard_map/all_to_all | solution.py:236
  465.9 18.3 %all_to_all.45 = bf16[4,2,147,512]{3,1,2,0:T(2,128)(2,1)S(1)} all-to-all(bf16[4,2,147,512]{3,1,2,0:T(2,128)(2,1)S(1)} %copy.321), channel_id=1, replica_groups=mesh['dp'=8,'expert'=4] {'expert'}, dimensions={0} | all-to-all | bytes 2408448 | tf_op jit(solution)/shard_map/all_to_all | solution.py:222
  504.3 11.1 %all-to-all-done.7 = bf16[4,2,147,512]{3,1,2,0:T(2,128)(2,1)} async-done(((bf16[4,2,147,512]{3,1,2,0:T(2,128)(2,1)}), bf16[4,2,147,512]{3,1,2,0:T(2,128)(2,1)}, u32[]{:S(2)}, u32[]{:S(2)}) %all-to-all-start.7) | async-done | bytes 1204256 | tf_op jit(solution)/shard_map/all_to_all | solution.py:236
  568.0 35.3 %reduce-scatter.37.cloned.1.call-done = bf16[64,1536]{1,0:T(8,128)(2,1)} async-done(((bf16[512,1536]{1,0:T(8,128)(2,1)}), bf16[64,1536]{1,0:T(8,128)(2,1)}) %reduce-scatter.37.cloned.1.call-update) | async-done | bytes 196624 | tf_op jit(solution)/shard_map/reduce_scatter | solution.py:344
  603.3 34.7 %reduce-scatter.35.cloned.1.call-done = bf16[64,1536]{1,0:T(8,128)(2,1)} async-done(((bf16[512,1536]{1,0:T(8,128)(2,1)}), bf16[64,1536]{1,0:T(8,128)(2,1)}) %reduce-scatter.35.cloned.1.call-update) | async-done | bytes 196624 | tf_op jit(solution)/shard_map/reduce_scatter | solution.py:344
  675.7 25.1 %reduce-scatter.53.cloned.1.call-done = bf16[64,2]{1,0:T(8,128)(2,1)} async-done(((bf16[512,2]{1,0:T(8,128)(2,1)}), bf16[64,2]{1,0:T(8,128)(2,1)}) %reduce-scatter.53.cloned.1.call-update) | async-done | bytes 272
  701.6 30.7 %reduce-scatter.49.cloned.1.call-done = bf16[64,2]{1,0:T(8,128)(2,1)} async-done(((bf16[512,2]{1,0:T(8,128)(2,1)}), bf16[64,2]{1,0:T(8,128)(2,1)}) %reduce-scatter.49.cloned.1.call-update) | async-done | bytes 272
  733.1 30.7 %reduce-scatter.43.cloned.1.call-done = bf16[64,8]{1,0:T(8,128)(2,1)} async-done(((bf16[512,8]{1,0:T(8,128)(2,1)}), bf16[64,8]{1,0:T(8,128)(2,1)}) %reduce-scatter.43.cloned.1.call-update) | async-done | bytes 1040
  766.5 28.1 %reduce-scatter.51.cloned.1.call-done = bf16[64,2]{1,0:T(8,128)(2,1)} async-done(((bf16[512,2]{1,0:T(8,128)(2,1)}), bf16[64,2]{1,0:T(8,128)(2,1)}) %reduce-scatter.51.cloned.1.call-update) | async-done | bytes 272
  795.4 30.7 %reduce-scatter.47.cloned.1.call-done = bf16[64,2]{1,0:T(8,128)(2,1)} async-done(((bf16[512,2]{1,0:T(8,128)(2,1)}), bf16[64,2]{1,0:T(8,128)(2,1)}) %reduce-scatter.47.cloned.1.call-update) | async-done | bytes 272
  826.8 10.1 all-reduce.2
  838.7 34.4 %all-reduce.6.cloned.1.call-done = (bf16[64,1536]{1,0:T(8,128)(2,1)}, bf16[64,1536]{1,0:T(8,128)(2,1)}, bf16[64,512]{1,0:T(8,128)(2,1)}, bf16[64,512]{1,0:T(8,128)(2,1)}) async-done(((bf16[64,1536]{1,0:T(8,128)(2,1)}, bf16[64,1536]{1,0:T(8,128)(2,1)}, bf16[64,512]{1,0:T(8,128)(2,1)}, bf16[64,512]{1,0:T(8,128)(2,1)}), (bf16[64,1536]{1,0:T(8,128)(2,1)}, bf16[64,1536]{1,0:T(8,128)(2,1)}, ...) | async-done | bytes 524304 | tf_op jit(solution)/shard_map/psum | solution.py:337
  876.6 48.5 %reduce-scatter.33.cloned.1.call-done = bf16[2,256,512]{2,1,0:T(8,128)(2,1)} async-done(((bf16[2,2048,512]{2,1,0:T(8,128)(2,1)}), bf16[2,256,512]{2,1,0:T(8,128)(2,1)}) %reduce-scatter.33.cloned.1.call-update) | async-done | bytes 524304 | tf_op jit(solution)/shard_map/reduce_scatter | solution.py:364
  925.1 50.7 %reduce-scatter.31.cloned.1.call-done = bf16[2,256,512]{2,1,0:T(8,128)(2,1)} async-done(((bf16[2,2048,512]{2,1,0:T(8,128)(2,1)}), bf16[2,256,512]{2,1,0:T(8,128)(2,1)}) %reduce-scatter.31.cloned.1.call-update) | async-done | bytes 524304 | tf_op jit(solution)/shard_map/reduce_scatter | solution.py:364
  978.5 47.9 %reduce-scatter.29.cloned.1.call-done = bf16[2,512,256]{2,1,0:T(8,128)(2,1)} async-done(((bf16[2,512,2048]{2,1,0:T(8,128)(2,1)}), bf16[2,512,256]{2,1,0:T(8,128)(2,1)}) %reduce-scatter.29.cloned.1.call-update) | async-done | bytes 524304 | tf_op jit(solution)/shard_map/reduce_scatter | solution.py:361
  1026.4 50.7 %reduce-scatter.27.cloned.1.call-done = bf16[2,512,256]{2,1,0:T(8,128)(2,1)} async-done(((bf16[2,512,2048]{2,1,0:T(8,128)(2,1)}), bf16[2,512,256]{2,1,0:T(8,128)(2,1)}) %reduce-scatter.27.cloned.1.call-update) | async-done | bytes 524304 | tf_op jit(solution)/shard_map/reduce_scatter | solution.py:361
  (623 shorter events, 427.3 us)
Async XLA Ops:
  7.2 113.5 %all-gather.19.cloned.1.call-start = ((), (), s32[]{:S(2)}) async-start(), calls=%async_computation.26 | async-start | bytes 1769472 | tf_op jit(solution)/shard_map/all_gather | solution.py:75
  9.1 172.9 %all-gather.21.cloned.1.call-start = ((), (), s32[]{:S(2)}) async-start(), calls=%async_computation.27 | async-start | bytes 4718592 | tf_op jit(solution)/shard_map/all_gather | solution.py:82
  11.4 180.0 %all-gather.23.cloned.1.call-start = ((), (), s32[]{:S(2)}) async-start(), calls=%async_computation.28 | async-start | bytes 4718592 | tf_op jit(solution)/shard_map/all_gather | solution.py:83
  12.6 224.3 %all-gather.25.cloned.1.call-start = ((), (), s32[]{:S(2)}) async-start(), calls=%async_computation.29 | async-start | bytes 1769472 | tf_op jit(solution)/shard_map/all_gather | solution.py:75
  13.2 288.6 %all-gather.27.cloned.1.call-start = ((), (), s32[]{:S(2)}) async-start(), calls=%async_computation.30 | async-start | bytes 4718592 | tf_op jit(solution)/shard_map/all_gather | solution.py:82
  13.8 297.1 %all-gather.29.cloned.1.call-start = ((), (), s32[]{:S(2)}) async-start(), calls=%async_computation.31 | async-start | bytes 4718592 | tf_op jit(solution)/shard_map/all_gather | solution.py:83
  14.5 67.9 %collective-permute-start = (bf16[1,64,512]{2,1,0:T(8,128)(2,1)S(1)}, bf16[1,64,512]{2,1,0:T(8,128)(2,1)S(1)}, u32[]{:S(2)}, u32[]{:S(2)}) collective-permute-start(bf16[1,64,512]{2,1,0:T(8,128)(2,1)S(1)} %get-tuple-element.130), channel_id=1, source_target_pairs={{0,4},{4,0},{8,12},{12,8},{16,20},{20,16},{24,28},{28,24},{1,5},{5... | collective-permute-start | bytes 196616 | tf_op jit(solution)/shard_map/ppermute | solution.py:26
  15.0 141.1 %collective-permute-start.3 = (bf16[1,64,512]{2,1,0:T(8,128)(2,1)}, bf16[1,64,512]{2,1,0:T(8,128)(2,1)}, u32[]{:S(2)}, u32[]{:S(2)}) collective-permute-start(bf16[1,64,512]{2,1,0:T(8,128)(2,1)} %get-tuple-element.129), channel_id=1, source_target_pairs={{0,4},{4,0},{8,12},{12,8},{16,20},{20,16},{24,28},{28,24},{1,5},{5... | collective-permute-start | bytes 196616 | tf_op jit(solution)/shard_map/ppermute | solution.py:26
  181.4 31.8 %collective-permute-start.5 = (bf16[4,64,512]{2,1,0:T(8,128)(2,1)S(1)}, bf16[4,64,512]{2,1,0:T(8,128)(2,1)}, u32[]{:S(2)}, u32[]{:S(2)}) collective-permute-start(bf16[4,64,512]{2,1,0:T(8,128)(2,1)S(1)} %bitcast.306), channel_id=1, source_target_pairs={{0,16},{4,20},{8,24},{12,28},{16,0},{20,4},{24,8},{28,12},{1,17},{... | collective-permute-start | bytes 786440 | tf_op jit(solution)/shard_map/ppermute | solution.py:26
  501.6 62.5 %reduce-scatter.41.cloned.1.call-start = ((), (), s32[]{:S(2)}) async-start(), calls=%async_computation.35 | async-start | bytes 589824 | tf_op jit(solution)/shard_map/reduce_scatter | solution.py:347
  504.2 63.8 %reduce-scatter.39.cloned.1.call-start = ((), (), s32[]{:S(2)}) async-start(), calls=%async_computation.34 | async-start | bytes 589824 | tf_op jit(solution)/shard_map/reduce_scatter | solution.py:347
  526.6 76.7 %reduce-scatter.37.cloned.1.call-start = ((), (), s32[]{:S(2)}) async-start(), calls=%async_computation.33 | async-start | bytes 1769472 | tf_op jit(solution)/shard_map/reduce_scatter | solution.py:344
  530.8 107.3 %reduce-scatter.35.cloned.1.call-start = ((), (), s32[]{:S(2)}) async-start(), calls=%async_computation.32 | async-start | bytes 1769472 | tf_op jit(solution)/shard_map/reduce_scatter | solution.py:344
  554.8 118.8 %reduce-scatter.45.cloned.1.call-start = ((), (), s32[]{:S(2)}) async-start(), calls=%async_computation.37 | async-start | bytes 147456
  555.9 144.9 %reduce-scatter.53.cloned.1.call-start = ((), (), s32[]{:S(2)}) async-start(), calls=%async_computation.41 | async-start | bytes 147456
  556.8 175.5 %reduce-scatter.49.cloned.1.call-start = ((), (), s32[]{:S(2)}) async-start(), calls=%async_computation.39 | async-start | bytes 147456
  557.7 206.0 %reduce-scatter.43.cloned.1.call-start = ((), (), s32[]{:S(2)}) async-start(), calls=%async_computation.36 | async-start | bytes 147456
  558.7 235.9 %reduce-scatter.51.cloned.1.call-start = ((), (), s32[]{:S(2)}) async-start(), calls=%async_computation.40 | async-start | bytes 147456
  563.1 263.0 %reduce-scatter.47.cloned.1.call-start = ((), (), s32[]{:S(2)}) async-start(), calls=%async_computation.38 | async-start | bytes 147456
  564.0 309.1 %all-reduce.6.cloned.1.call-start = ((), (), s32[]{:S(2)}) async-start(), calls=%async_computation.42 | async-start | bytes 1048576 | tf_op jit(solution)/shard_map/psum | solution.py:337
  638.1 287.0 %reduce-scatter.33.cloned.1.call-start = ((), (), s32[]{:S(2)}) async-start(), calls=%async_computation.25 | async-start | bytes 4718592 | tf_op jit(solution)/shard_map/reduce_scatter | solution.py:364
  646.7 329.1 %reduce-scatter.31.cloned.1.call-start = ((), (), s32[]{:S(2)}) async-start(), calls=%async_computation.24 | async-start | bytes 4718592 | tf_op jit(solution)/shard_map/reduce_scatter | solution.py:364
  656.5 369.9 %reduce-scatter.29.cloned.1.call-start = ((), (), s32[]{:S(2)}) async-start(), calls=%async_computation.23 | async-start | bytes 4718592 | tf_op jit(solution)/shard_map/reduce_scatter | solution.py:361
  665.0 412.2 %reduce-scatter.27.cloned.1.call-start = ((), (), s32[]{:S(2)}) async-start(), calls=%async_computation.22 | async-start | bytes 4718592 | tf_op jit(solution)/shard_map/reduce_scatter | solution.py:361
  (151 other events, 1436.1 us)
Sparse Core Ops, SparseCore 0:
  10.2 29.3 all-gather.18
  41.2 51.1 all-gather.20
  94.0 50.2 all-gather.22
  146.4 27.8 all-gather.24
  175.7 59.1 all-gather.26
  236.3 46.7 all-gather.28
  504.7 31.5 reduce-scatter.40
  538.5 29.4 reduce-scatter.38
  570.9 32.3 reduce-scatter.36
  605.5 32.5 reduce-scatter.34
  640.9 28.9 reduce-scatter.44
  672.0 28.7 reduce-scatter.52
  703.6 28.6 reduce-scatter.48
  735.0 28.7 reduce-scatter.42
  765.8 28.7 reduce-scatter.50
  797.3 28.7 reduce-scatter.46
  829.1 43.8 all-reduce.5
  875.2 49.8 reduce-scatter.32
  927.4 48.3 reduce-scatter.30
  978.0 48.3 reduce-scatter.28
  1028.7 48.3 reduce-scatter.26
